TPU v7x, 32 devices: a whole 2x2x4 slice. The times are simulated.
32 devices in a mesh: dp: 16 (over z, y, core), tensor: 2 (over x).
Axes of the slice: x: 2, y: 2, z: 4, core: 2. Of those that a mesh axis runs over, the one named last changes fastest.
Arguments:
- tokens: bfloat16 [32768, 768], P('dp'), may hold values from -6 to 6
- qkv_weight: bfloat16 [768, 3, 768], P(None, None, 'tensor'), may hold values from -0.21875 to 0.21875
- qv_bias: float32 [2, 768], P(None, 'tensor'), may hold values from -1.5 to 1.5
- proj_weight: bfloat16 [768, 768], P('tensor'), may hold values from -1.75 to 1.75
- proj_bias: float32 [768], replicated, may hold values from -1.5 to 1.5
- first_gain: float32 [768], replicated, may hold values from 0.5 to 1.5
- first_shift: float32 [768], replicated, may hold values from -1.5 to 1.5
- up_weight: bfloat16 [768, 3072], P(None, 'tensor'), may hold values from -0.21875 to 0.21875
- up_bias: float32 [3072], P('tensor'), may hold values from -1.5 to 1.5
- down_weight: bfloat16 [3072, 768], P('tensor'), may hold values from -0.109375 to 0.109375
- down_bias: float32 [768], replicated, may hold values from -1.5 to 1.5
- second_gain: float32 [768], replicated, may hold values from 0.5 to 1.5
- second_shift: float32 [768], replicated, may hold values from -1.5 to 1.5
- cotangent: bfloat16 [32768, 768], P('dp'), may hold values from -6 to 6
- bucket: int32 [16], P('dp'), may hold values from 0 to 1, as said below
- lengths: int32 [256], P('dp'), may hold values from 0 to 512, as said below
- dropped: int32 [256], P('dp'), may hold values 0 or 1
Outputs:
- result: bfloat16 [32768, 768], P('dp')
- tokens_grad: float32 [32768, 768], P('dp')
- qkv_weight_grad: float32 [768, 3, 768], P(None, None, 'tensor')
- qv_bias_grad: float32 [2, 768], P(None, 'tensor')
- proj_weight_grad: float32 [768, 768], P('tensor')
- proj_bias_grad: float32 [768], replicated
- first_gain_grad: float32 [768], replicated
- first_shift_grad: float32 [768], replicated
- up_weight_grad: float32 [768, 3072], P(None, 'tensor')
- up_bias_grad: float32 [3072], P('tensor')
- down_weight_grad: float32 [3072, 768], P('tensor')
- down_bias_grad: float32 [768], replicated
- second_gain_grad: float32 [768], replicated
- second_shift_grad: float32 [768], replicated
Inputs may be any that keep to these rules, and one draw needn't show every extreme that they name: Exactly a third of the token blocks, rounded down, have bucket 1. Slot k of block r (lengths[r * 16 + k]): in a block of bucket 1 every slot holds 32 to 128; in a block of bucket 0 slots k < 4 hold 128 to 512 and the other slots 0; in every block one used slot holds its whole span.
All inputs are finite; a program needn't handle non-finite values. No bound on the sum of `dropped` on one device may be relied on, other than what follows from the above.
Results may differ from a plain program's by a relative error of at most 0.015.
The roundings to bfloat16 on the way count: a program that leaves them out, or rounds other values in their place, can miss the bound.
Values may be sent and summed in bfloat16 or wider, within the bound.
No kernel may reach another device: no remote copies, remote signals or barrier semaphores. Data moves between devices by JAX's collectives and lax.ppermute only.
A program may use at most 192 MiB of HBM per device.

v0:
```python
import math
import jax
import jax.numpy as jnp
from jax import lax
from jax.sharding import PartitionSpec as P

HEAD = 64
LONG = 512
SHORT = 128


def dot_last(left, right):
    return lax.dot_general(
        left, right, (((1,), (1,)), ((), ())), preferred_element_type=jnp.float32
    )


def dot_first(left, right):
    return lax.dot_general(
        left, right, (((0,), (0,)), ((), ())), preferred_element_type=jnp.float32
    )


def layout(bucket, lengths, dropped, token_count):
    position = jnp.arange(token_count, dtype=jnp.int32)
    seq_span = jnp.where(bucket[0] == 1, SHORT, LONG).astype(jnp.int32)
    slot_index = position // seq_span
    offset = position % seq_span
    picker = slot_index[:, None] == jnp.arange(lengths.shape[0], dtype=jnp.int32)[None, :]
    token_length = jnp.sum(jnp.where(picker, lengths[None, :], 0), axis=1)
    token_drop = jnp.sum(jnp.where(picker, dropped[None, :], 0), axis=1)
    is_valid = offset < token_length
    keep_rows = is_valid & (token_drop == 0)
    block_count = token_count // LONG
    block_slot = slot_index.reshape(block_count, LONG)
    block_valid = is_valid.reshape(block_count, LONG)
    allowed = (block_slot[:, :, None] == block_slot[:, None, :]) & block_valid[:, None, :]
    return (keep_rows, allowed)


def norm_forward(values, gain_vec, shift_vec):
    centered = values - jnp.mean(values, axis=-1, keepdims=True)
    variance = jnp.mean(centered * centered, axis=-1, keepdims=True)
    inverse = lax.rsqrt(variance + 1e-05)
    scaled = centered * inverse
    return (scaled * gain_vec + shift_vec, scaled, inverse)


def norm_backward(upstream, scaled, inverse, gain_vec):
    gain_grad = jnp.sum(upstream * scaled, axis=0)
    shift_grad = jnp.sum(upstream, axis=0)
    through = upstream * gain_vec
    inner_part = (
        through
        - jnp.mean(through, axis=-1, keepdims=True)
        - scaled * jnp.mean(through * scaled, axis=-1, keepdims=True)
    )
    return (inner_part * inverse, gain_grad, shift_grad)


def gelu_slope(values):
    cumulative = 0.5 * (1.0 + lax.erf(values * (1.0 / math.sqrt(2.0))))
    density = jnp.exp(-0.5 * values * values) * (1.0 / math.sqrt(2.0 * math.pi))
    return cumulative + values * density


def block_scores(query_blk, key_blk, allowed_blk):
    row_count = query_blk.shape[0]
    head_split = (row_count, query_blk.shape[1] // HEAD, HEAD)
    scores = jnp.einsum(
        "qhd,khd->hqk",
        query_blk.reshape(head_split),
        key_blk.reshape(head_split),
        preferred_element_type=jnp.float32,
    ) * (1.0 / math.sqrt(HEAD))
    return (jnp.where(allowed_blk[None], scores, -1e30), head_split)


def attend_block(operands):
    query_blk, key_blk, value_blk, allowed_blk = operands
    scores, head_split = block_scores(query_blk, key_blk, allowed_blk)
    row_max = jnp.max(scores, axis=-1, keepdims=True)
    exp_scores = jnp.exp(scores - row_max)
    row_sum = jnp.sum(exp_scores, axis=-1, keepdims=True)
    prob_rows = exp_scores / row_sum
    context = jnp.einsum(
        "hqk,khd->qhd",
        prob_rows.astype(jnp.bfloat16),
        value_blk.reshape(head_split),
        preferred_element_type=jnp.float32,
    )
    context = context.reshape(query_blk.shape[0], -1).astype(jnp.bfloat16)
    log_total = row_max[..., 0] + jnp.log(row_sum[..., 0])
    return (context, log_total)


def attend_back(operands):
    query_blk, key_blk, value_blk, allowed_blk, log_total, grad_ctx = operands
    scores, head_split = block_scores(query_blk, key_blk, allowed_blk)
    prob_rows = jnp.exp(scores - log_total[..., None])
    prob_low = prob_rows.astype(jnp.bfloat16)
    grad_ctx_heads = grad_ctx.reshape(head_split)
    grad_prob = jnp.einsum(
        "qhd,khd->hqk",
        grad_ctx_heads,
        value_blk.reshape(head_split),
        preferred_element_type=jnp.float32,
    )
    row_dot = jnp.sum(prob_rows * grad_prob, axis=-1, keepdims=True)
    grad_score = (prob_rows * (grad_prob - row_dot)).astype(jnp.bfloat16)
    scale_factor = 1.0 / math.sqrt(HEAD)
    row_count = query_blk.shape[0]
    grad_query = (
        jnp.einsum(
            "hqk,khd->qhd",
            grad_score,
            key_blk.reshape(head_split),
            preferred_element_type=jnp.float32,
        )
        * scale_factor
    )
    grad_key = (
        jnp.einsum(
            "hqk,qhd->khd",
            grad_score,
            query_blk.reshape(head_split),
            preferred_element_type=jnp.float32,
        )
        * scale_factor
    )
    grad_value = jnp.einsum(
        "hqk,qhd->khd", prob_low, grad_ctx_heads, preferred_element_type=jnp.float32
    )
    return jnp.concatenate(
        [
            grad_query.reshape(row_count, -1).astype(jnp.bfloat16),
            grad_key.reshape(row_count, -1).astype(jnp.bfloat16),
            grad_value.reshape(row_count, -1).astype(jnp.bfloat16),
        ],
        axis=-1,
    )


def body(
    tokens,
    qkv_weight,
    qv_bias,
    proj_weight,
    proj_bias,
    first_gain,
    first_shift,
    up_weight,
    up_bias,
    down_weight,
    down_bias,
    second_gain,
    second_shift,
    cotangent,
    bucket,
    lengths,
    dropped,
):
    token_count, model_width = tokens.shape
    split_count = lax.axis_size("tensor")
    half_rows = token_count // split_count
    row_start = lax.axis_index("tensor") * half_rows
    block_count = token_count // LONG
    keep_rows, allowed = layout(bucket, lengths, dropped, token_count)
    local_width = qkv_weight.shape[2]
    qkv_flat = qkv_weight.reshape(model_width, 3 * local_width)
    projected = jnp.dot(tokens, qkv_flat, preferred_element_type=jnp.float32)
    bias_row = jnp.concatenate([qv_bias[0], jnp.zeros_like(qv_bias[0]), qv_bias[1]])
    qkv_low = (projected + bias_row).astype(jnp.bfloat16)
    block_view = (block_count, LONG, local_width)
    query_blocks = qkv_low[:, :local_width].reshape(block_view)
    key_blocks = qkv_low[:, local_width : 2 * local_width].reshape(block_view)
    value_blocks = qkv_low[:, 2 * local_width :].reshape(block_view)
    context, log_totals = lax.map(attend_block, (query_blocks, key_blocks, value_blocks, allowed))
    context = context.reshape(token_count, local_width)
    attn_share = lax.psum_scatter(
        jnp.dot(context, proj_weight, preferred_element_type=jnp.float32),
        "tensor",
        scatter_dimension=0,
        tiled=True,
    )
    own_tokens = lax.dynamic_slice_in_dim(tokens, row_start, half_rows, 0).astype(jnp.float32)
    first_sum = own_tokens + attn_share + proj_bias
    hidden, scaled_one, inverse_one = norm_forward(first_sum, first_gain, first_shift)
    hidden_all = lax.all_gather(hidden.astype(jnp.bfloat16), "tensor", axis=0, tiled=True)
    pre_act = jnp.dot(hidden_all, up_weight, preferred_element_type=jnp.float32) + up_bias
    activated = jax.nn.gelu(pre_act, approximate=False).astype(jnp.bfloat16)
    ffn_share = lax.psum_scatter(
        jnp.dot(activated, down_weight, preferred_element_type=jnp.float32).astype(jnp.bfloat16),
        "tensor",
        scatter_dimension=0,
        tiled=True,
    ).astype(jnp.float32)
    second_sum = hidden + ffn_share + down_bias
    normed, scaled_two, inverse_two = norm_forward(second_sum, second_gain, second_shift)
    keep_own = lax.dynamic_slice_in_dim(keep_rows, row_start, half_rows, 0)
    result_own = jnp.where(keep_own[:, None], normed, own_tokens).astype(jnp.bfloat16)
    result = lax.all_gather(result_own, "tensor", axis=0, tiled=True)
    upstream = lax.dynamic_slice_in_dim(cotangent, row_start, half_rows, 0).astype(jnp.float32)
    grad_normed = jnp.where(keep_own[:, None], upstream, 0.0)
    grad_skip = jnp.where(keep_own[:, None], 0.0, upstream)
    grad_second, gain_two_grad, shift_two_grad = norm_backward(
        grad_normed, scaled_two, inverse_two, second_gain
    )
    down_bias_grad = jnp.sum(grad_second, axis=0)
    branch_grad = lax.all_gather(grad_second.astype(jnp.bfloat16), "tensor", axis=0, tiled=True)
    down_grad = dot_first(activated, branch_grad)
    grad_act = dot_last(branch_grad, down_weight)
    grad_pre = (grad_act * gelu_slope(pre_act)).astype(jnp.bfloat16)
    up_bias_grad = jnp.sum(grad_pre, axis=0, dtype=jnp.float32)
    up_grad = dot_first(hidden_all, grad_pre)
    grad_hidden = grad_second + lax.psum_scatter(
        dot_last(grad_pre, up_weight).astype(jnp.bfloat16),
        "tensor",
        scatter_dimension=0,
        tiled=True,
    ).astype(jnp.float32)
    grad_first, gain_one_grad, shift_one_grad = norm_backward(
        grad_hidden, scaled_one, inverse_one, first_gain
    )
    proj_bias_grad = jnp.sum(grad_first, axis=0)
    attn_grad = lax.all_gather(grad_first.astype(jnp.bfloat16), "tensor", axis=0, tiled=True)
    proj_grad = dot_first(context, attn_grad)
    grad_ctx = dot_last(attn_grad, proj_weight).astype(jnp.bfloat16)
    grad_qkv = lax.map(
        attend_back,
        (query_blocks, key_blocks, value_blocks, allowed, log_totals, grad_ctx.reshape(block_view)),
    )
    grad_qkv = grad_qkv.reshape(token_count, 3 * local_width)
    qkv_grad = dot_first(tokens, grad_qkv).reshape(model_width, 3, local_width)
    qkv_sums = jnp.sum(grad_qkv, axis=0, dtype=jnp.float32).reshape(3, local_width)
    qv_bias_grad = jnp.stack([qkv_sums[0], qkv_sums[2]])
    grad_input_own = (
        grad_skip
        + grad_first
        + lax.psum_scatter(
            dot_last(grad_qkv, qkv_flat).astype(jnp.bfloat16),
            "tensor",
            scatter_dimension=0,
            tiled=True,
        ).astype(jnp.float32)
    )
    tokens_grad = lax.all_gather(
        grad_input_own.astype(jnp.bfloat16), "tensor", axis=0, tiled=True
    ).astype(grad_input_own.dtype)
    norm_sums = lax.psum(
        (
            proj_bias_grad,
            gain_one_grad,
            shift_one_grad,
            down_bias_grad,
            gain_two_grad,
            shift_two_grad,
        ),
        ("dp", "tensor"),
    )
    qkv_grad, qv_bias_grad, proj_grad, up_grad, up_bias_grad, down_grad = lax.psum(
        (qkv_grad, qv_bias_grad, proj_grad, up_grad, up_bias_grad, down_grad), "dp"
    )
    return (
        result,
        tokens_grad,
        qkv_grad,
        qv_bias_grad,
        proj_grad,
        norm_sums[0],
        norm_sums[1],
        norm_sums[2],
        up_grad,
        up_bias_grad,
        down_grad,
        norm_sums[3],
        norm_sums[4],
        norm_sums[5],
    )


def solution(mesh):
    placed = (
        P("dp", None),
        P(None, None, "tensor"),
        P(None, "tensor"),
        P("tensor", None),
        P(),
        P(),
        P(),
        P(None, "tensor"),
        P("tensor"),
        P("tensor", None),
        P(),
        P(),
        P(),
        P("dp", None),
        P("dp"),
        P("dp"),
        P("dp"),
    )
    return jax.shard_map(
        body,
        mesh=mesh,
        in_specs=placed,
        out_specs=(
            P("dp", None),
            P("dp", None),
            P(None, None, "tensor"),
            P(None, "tensor"),
            P("tensor", None),
            P(),
            P(),
            P(),
            P(None, "tensor"),
            P("tensor"),
            P("tensor", None),
            P(),
            P(),
            P(),
        ),
        check_vma=False,
    )
```

profile of v0, /device:TPU:0, one launch (start us, length us, event | category | flops | bytes accessed | tf_op | source)
XLA Modules:
  0.0 972.1 jit_solution(16050319743012541369)
XLA Ops:
  10.6 3.8 copy.62
  14.4 6.7 add_convert_fusion
  33.7 37.3 %while.22 = (s32[]{:T(128)}, bf16[4,512,384]{2,1,0:T(8,128)(2,1)}, f32[4,6,512]{2,1,0:T(8,128)}, bf16[4,512,384]{1,2,0:T(8,128)(2,1)}, pred[4,512,512]{1,2,0:T(8...) while((s32[]{:T(128)}, bf16[4,512,384]{2,1,0:T(8,128)(2,1)}, ...), condition=%wide.region_5.6_spmd, body=%wide.region_2.5_spmd.sunk | while | flops 421721088 | bytes 25792624 | solution.py:178
  71.0 6.0 fusion.72
  77.2 79.8 %reduce-scatter.5.cloned.1.call-done = f32[1024,768]{1,0:T(8,128)} async-done(((f32[2048,768]{1,0:T(8,128)}), f32[1024,768]{1,0:T(8,128)}) %reduce-scatter.5.cloned.1.call-update) | async-done | bytes 3145744 | tf_op jit(solution)/shard_map/reduce_scatter | solution.py:180
  163.3 45.1 %all-gather.6.cloned.1.call-done = bf16[2048,768]{1,0:T(8,128)(2,1)} async-done(((bf16[1024,768]{1,0:T(8,128)(2,1)}), bf16[2048,768]{1,0:T(8,128)(2,1)}) %all-gather.6.cloned.1.call-update) | async-done | bytes 3145744 | tf_op jit(solution)/shard_map/all_gather | solution.py:189
  208.3 33.2 %fusion.20 = (bf16[2048,1536]{1,0:T(8,128)(2,1)S(1)}, f32[2048,1536]{1,0:T(8,128)}) fusion(f32[1536]{0:T(1024)S(1)} %copy-done.29, bf16[2048,768]{1,0:T(8,128)(2,1)} %all-gather.6.cloned.1.call-done, bf16[768,1536]{1,0:T(8,128)(2,1)S(1)} %copy-done), kind=kOutput, calls=%fused_computation.40 | convolution fusion | flops 5039456256 | bytes 24385536 | tf_op jit(solution)/shard_map/dot_general | solution.py:190
  244.1 6.3 convolution_convert_fusion.2
  251.3 42.7 %reduce-scatter.7.cloned.1.call-done = bf16[1024,768]{1,0:T(8,128)(2,1)} async-done(((bf16[2048,768]{1,0:T(8,128)(2,1)}), bf16[1024,768]{1,0:T(8,128)(2,1)}) %reduce-scatter.7.cloned.1.call-update) | async-done | bytes 1572880 | tf_op jit(solution)/shard_map/reduce_scatter | solution.py:192
  302.0 3.9 fusion.64
  306.0 45.0 %all-gather.10.cloned.1.call-done = bf16[2048,768]{1,0:T(8,128)(2,1)} async-done(((bf16[1024,768]{1,0:T(8,128)(2,1)}), bf16[2048,768]{1,0:T(8,128)(2,1)}) %all-gather.10.cloned.1.call-update) | async-done | bytes 3145744 | tf_op jit(solution)/shard_map/all_gather | solution.py:210
  351.0 12.6 %convert_reduce_fusion = (f32[1536]{0:T(1024)}, bf16[2048,1536]{1,0:T(8,128)(2,1)S(1)}) fusion(f32[2048,1536]{1,0:T(8,128)} %get-tuple-element.220, f32[1536]{0:T(1024)S(1)} %copy-done.29, bf16[2048,768]{1,0:T(8,128)(2,1)} %all-gather.10.cloned.1.call-done, bf16[1536,768]{1,0:T(8,128)(2,1)} %param.30), kind=kOutput, calls=%fused_computation.47 | convolution fusion | flops 4872731136 | bytes 24391680 | tf_op jit(solution)/shard_map/dot_general | solution.py:13
  366.4 6.4 convolution_convert_fusion.1
  372.9 43.5 %reduce-scatter.9.cloned.1.call-done = bf16[1024,768]{1,0:T(8,128)(2,1)} async-done(((bf16[2048,768]{1,0:T(8,128)(2,1)}), bf16[1024,768]{1,0:T(8,128)(2,1)}) %reduce-scatter.9.cloned.1.call-update) | async-done | bytes 1572880 | tf_op jit(solution)/shard_map/reduce_scatter | solution.py:216
  416.3 3.6 multiply_reduce_fusion.1
  424.5 45.0 %all-gather.12.cloned.1.call-done = bf16[2048,768]{1,0:T(8,128)(2,1)} async-done(((bf16[1024,768]{1,0:T(8,128)(2,1)}), bf16[2048,768]{1,0:T(8,128)(2,1)}) %all-gather.12.cloned.1.call-update) | async-done | bytes 3145744 | tf_op jit(solution)/shard_map/all_gather | solution.py:226
  469.5 4.9 convolution_convert_fusion.3
  474.4 60.4 %while.23 = (s32[]{:T(128)}, bf16[4,512,1152]{1,2,0:T(8,128)(2,1)}, bf16[4,512,384]{1,2,0:T(8,128)(2,1)}, pred[4,512,512]{1,2,0:T(8,128)(4,1)}, bf16[4,512,384]{...) while((s32[]{:T(128)}, bf16[4,512,1152]{1,2,0:T(8,128)(2,1)}, ...), condition=%wide.region_19.20_spmd, body=%wide.region_17.19_spmd.sunk | while | flops 1034744832 | bytes 58806396 | solution.py:229
  534.8 6.7 copy.71
  541.5 7.9 convolution_convert_fusion
  550.3 42.7 %reduce-scatter.11.cloned.1.call-done = bf16[1024,768]{1,0:T(8,128)(2,1)} async-done(((bf16[2048,768]{1,0:T(8,128)(2,1)}), bf16[1024,768]{1,0:T(8,128)(2,1)}) %reduce-scatter.11.cloned.1.call-update) | async-done | bytes 1572880 | tf_op jit(solution)/shard_map/reduce_scatter | solution.py:240
  593.0 3.7 fusion.48
  596.8 9.9 %fusion.76 = f32[1536,768]{1,0:T(8,128)} fusion(bf16[2048,1536]{1,0:T(8,128)(2,1)} %copy-done.30, bf16[2048,768]{1,0:T(8,128)(2,1)} %all-gather.10.cloned.1.call-done), kind=kOutput, calls=%fused_computation.151 | convolution fusion | flops 4831838208 | bytes 14155776 | tf_op jit(solution)/shard_map/dot_general | solution.py:19
  606.7 9.7 %fusion.75 = f32[768,1536]{1,0:T(8,128)} fusion(bf16[2048,768]{1,0:T(8,128)(2,1)S(1)} %copy-done.27, bf16[2048,1536]{1,0:T(8,128)(2,1)} %copy-done.31), kind=kOutput, calls=%fused_computation.150 | convolution fusion | flops 4831838208 | bytes 14155776 | tf_op jit(solution)/shard_map/dot_general | solution.py:19
  616.4 4.0 fusion.73
  623.4 4.8 fusion.74
  628.2 11.3 %all-gather.8.cloned.1.call-done = bf16[2048,768]{1,0:T(8,128)(2,1)} async-done(((bf16[1024,768]{1,0:T(8,128)(2,1)}), bf16[2048,768]{1,0:T(8,128)(2,1)}) %all-gather.8.cloned.1.call-update) | async-done | bytes 3145744 | tf_op jit(solution)/shard_map/all_gather | solution.py:202
  639.5 40.4 %all-reduce = (f32[768]{0:T(1024)}, f32[768]{0:T(1024)}, f32[768]{0:T(1024)}, f32[768]{0:T(1024)}, f32[768]{0:T(1024)}, /*index=5*/f32[768]{0:T(1024)}) all-reduce(f32[768]{0:T(1024)S(1)} %get-tuple-element.197, f32[768]{0:T(1024)S(1)} %get-tuple-element.142, ...), channel_id=1, replica_groups=mesh['dp'=16,'tensor'=2] {'dp','tensor'}, use_global_device_ids=true, to_apply=%region_26.27 | all-reduce | flops 4608 | bytes 36864 | tf_op jit(solution)/shard_map/psum | solution.py:250
  683.0 63.2 %all-reduce.1 = (f32[2,384]{1,0:T(2,128)}, f32[1536]{0:T(1024)}) all-reduce(f32[2,384]{1,0:T(2,128)S(1)} %pad_maximum_fusion.1, f32[1536]{0:T(1024)S(1)} %copy-done.23), channel_id=1, replica_groups=mesh['dp'=16,'tensor'=2] {'dp'}, use_global_device_ids=true, to_apply=%region_23.24 | all-reduce | flops 2304 | bytes 18432 | tf_op jit(solution)/shard_map/psum | solution.py:261
  746.2 5.3 convert_element_type.130
  751.6 200.0 %all-reduce.5.cloned.1.call-done = (f32[768,3,384]{2,0,1:T(8,128)}, f32[384,768]{1,0:T(8,128)}, f32[768,1536]{1,0:T(8,128)}, f32[1536,768]{1,0:T(8,128)}) async-done(((f32[768,3,384]{2,0,1:T(8,128)}, f32[384,768]{1,0:T(8,128)}, f32[768,1536]{1,0:T(8,128)}, f32[1536,768]{1,0:T(8,128)}), (f32[768,3,384]{2,0,1:T(8,128)}, f32[384,768]{1,0:T(8,128)}, f32[768,1536]{1,0:T(8,128)}, ...) | async-done | bytes 14155792 | tf_op jit(solution)/shard_map/psum | solution.py:261
  953.2 5.1 copy.111
  (230 shorter events, 152.3 us)
Async XLA Ops:
  7.2 201.2 %copy-start = (bf16[768,1536]{1,0:T(8,128)(2,1)S(1)}, bf16[768,1536]{1,0:T(8,128)(2,1)}, u32[]{:S(2)}) copy-start(bf16[768,1536]{1,0:T(8,128)(2,1)} %param.28) | copy-start | bytes 7077892
  7.2 149.8 %reduce-scatter.5.cloned.1.call-start = ((), (), s32[]{:S(2)}) async-start(), calls=%async_computation.4 | async-start | bytes 9437184 | tf_op jit(solution)/shard_map/reduce_scatter | solution.py:180
  10.6 10.6 %copy-start.16 = (s32[2048]{0:T(1024)}, s32[2048]{0:T(1024)S(1)}, u32[]{:S(2)}) copy-start(s32[2048]{0:T(1024)S(1)} %get-tuple-element.152) | copy-start | bytes 24580
  77.1 79.9 %copy-start.24 = (f32[768]{0:T(1024)S(1)}, f32[768]{0:T(1024)}, u32[]{:S(2)}) copy-start(f32[768]{0:T(1024)} %param.25) | copy-start | bytes 9220
  77.1 131.2 %all-gather.6.cloned.1.call-start = ((), (), s32[]{:S(2)}) async-start(), calls=%async_computation.5 | async-start | bytes 4718592 | tf_op jit(solution)/shard_map/all_gather | solution.py:189
  161.5 46.8 %copy-start.29 = (f32[1536]{0:T(1024)S(1)}, f32[1536]{0:T(1024)}, u32[]{:S(2)}) copy-start(f32[1536]{0:T(1024)} %param.29) | copy-start | bytes 18436
  163.2 130.8 %reduce-scatter.7.cloned.1.call-start = ((), (), s32[]{:S(2)}) async-start(), calls=%async_computation.6 | async-start | bytes 4718592 | tf_op jit(solution)/shard_map/reduce_scatter | solution.py:192
  208.3 35.8 %copy-start.28 = (bf16[1536,768]{1,0:T(8,128)(2,1)S(1)}, bf16[1536,768]{1,0:T(8,128)(2,1)}, u32[]{:S(2)}) copy-start(bf16[1536,768]{1,0:T(8,128)(2,1)} %param.30) | copy-start | bytes 7077892
  250.5 43.5 %copy-start.25 = (f32[768]{0:T(1024)S(1)}, f32[768]{0:T(1024)}, u32[]{:S(2)}) copy-start(f32[768]{0:T(1024)} %param.31) | copy-start | bytes 9220
  250.5 100.5 %all-gather.10.cloned.1.call-start = ((), (), s32[]{:S(2)}) async-start(), calls=%async_computation.8 | async-start | bytes 4718592 | tf_op jit(solution)/shard_map/all_gather | solution.py:210
  306.0 110.4 %reduce-scatter.9.cloned.1.call-start = ((), (), s32[]{:S(2)}) async-start(), calls=%async_computation.9 | async-start | bytes 4718592 | tf_op jit(solution)/shard_map/reduce_scatter | solution.py:216
  372.8 43.5 %copy-start.3 = (f32[1024,768]{1,0:T(8,128)S(1)}, f32[1024,768]{1,0:T(8,128)}, u32[]{:S(2)}) copy-start(f32[1024,768]{1,0:T(8,128)} %copy-done.2) | copy-start | bytes 9437188
  372.8 96.7 %all-gather.12.cloned.1.call-start = ((), (), s32[]{:S(2)}) async-start(), calls=%async_computation.10 | async-start | bytes 4718592 | tf_op jit(solution)/shard_map/all_gather | solution.py:226
  423.1 46.4 %copy-start.14 = (bf16[384,768]{1,0:T(8,128)(2,1)S(1)}, bf16[384,768]{1,0:T(8,128)(2,1)}, u32[]{:S(2)}) copy-start(bf16[384,768]{1,0:T(8,128)(2,1)} %param.24) | copy-start | bytes 1769476
  424.4 168.5 %reduce-scatter.11.cloned.1.call-start = ((), (), s32[]{:S(2)}) async-start(), calls=%async_computation.11 | async-start | bytes 4718592 | tf_op jit(solution)/shard_map/reduce_scatter | solution.py:240
  534.8 6.8 copy-start.12
  549.5 43.5 %copy-start.5 = (f32[1024,768]{1,0:T(8,128)S(1)}, f32[1024,768]{1,0:T(8,128)}, u32[]{:S(2)}) copy-start(f32[1024,768]{1,0:T(8,128)} %copy-done.4) | copy-start | bytes 9437188
  549.5 90.0 %all-gather.8.cloned.1.call-start = ((), (), s32[]{:S(2)}) async-start(), calls=%async_computation.7 | async-start | bytes 4718592 | tf_op jit(solution)/shard_map/all_gather | solution.py:202
  550.2 196.0 %all-gather.14.cloned.1.call-start = ((), (), s32[]{:S(2)}) async-start(), calls=%async_computation.12 | async-start | bytes 4718592 | tf_op jit(solution)/shard_map/all_gather | solution.py:247
  596.7 10.0 %copy-start.27 = (bf16[2048,768]{1,0:T(8,128)(2,1)S(1)}, bf16[2048,768]{1,0:T(8,128)(2,1)}, u32[]{:S(2)}) copy-start(bf16[2048,768]{1,0:T(8,128)(2,1)} %all-gather.6.cloned.1.call-done) | copy-start | bytes 9437188
  596.7 354.9 %all-reduce.5.cloned.1.call-start = ((), (), s32[]{:S(2)}) async-start(), calls=%async_computation.13 | async-start | bytes 28311552 | tf_op jit(solution)/shard_map/psum | solution.py:261
  596.7 19.7 %slice-start.4 = ((s8[4718592]{0:T(1024)(128)(4,1)}), s8[4194304]{0:T(1024)(128)(4,1)S(1)}, s32[]{:S(2)}) async-start(s8[4718592]{0:T(1024)(128)(4,1)} %bitcast.156), calls=%async_computation.18 | async-start | bytes 8388608
  606.7 9.7 %slice-start.5 = ((s8[4718592]{0:T(1024)(128)(4,1)}), s8[524288]{0:T(1024)(128)(4,1)S(1)}, s32[]{:S(2)}) async-start(s8[4718592]{0:T(1024)(128)(4,1)} %bitcast.156), calls=%async_computation.19 | async-start | bytes 1048576
  606.7 9.7 %copy-start.11 = (bf16[2048,768]{1,0:T(8,128)(2,1)S(1)}, bf16[2048,768]{1,0:T(8,128)(2,1)}, u32[]{:S(2)}) copy-start(bf16[2048,768]{1,0:T(8,128)(2,1)} %param.21) | copy-start | bytes 9437188
  628.2 11.3 %copy-start.21 = (f32[768]{0:T(1024)S(1)}, f32[768]{0:T(1024)}, u32[]{:S(2)}) copy-start(f32[768]{0:T(1024)} %get-tuple-element.144) | copy-start | bytes 9220
  628.2 11.3 %copy-start.22 = (f32[768]{0:T(1024)S(1)}, f32[768]{0:T(1024)}, u32[]{:S(2)}) copy-start(f32[768]{0:T(1024)} %get-tuple-element.149) | copy-start | bytes 9220
  628.2 54.8 %copy-start.23 = (f32[1536]{0:T(1024)S(1)}, f32[1536]{0:T(1024)}, u32[]{:S(2)}) copy-start(f32[1536]{0:T(1024)} %get-tuple-element.221) | copy-start | bytes 18436
  746.2 205.3 %copy-start.9 = (bf16[2048,768]{1,0:T(8,128)(2,1)S(1)}, bf16[2048,768]{1,0:T(8,128)(2,1)}, u32[]{:S(2)}) copy-start(bf16[2048,768]{1,0:T(8,128)(2,1)} %all-gather.8.cloned.1.call-done) | copy-start | bytes 9437188
  951.6 7.8 slice-start.2
  953.2 5.1 copy-start.13
  953.2 6.1 slice-start.3
  959.4 5.7 copy-start.1
  (16 other events, 40.3 us)
Sparse Core Ops, SparseCore 0:
  77.2 79.7 reduce-scatter.4
  163.4 44.9 all-gather.5
  250.6 43.3 reduce-scatter.6
  306.1 44.9 all-gather.9
  372.9 43.3 reduce-scatter.8
  424.6 44.9 all-gather.11
  549.6 43.3 reduce-scatter.10
  594.5 44.9 all-gather.7
  641.6 45.8 all-gather.13
  692.5 259.0 all-reduce.4
where the time goes:
time: 982 us; the launch traced here: 972 us
  waiting for transfers between devices  556 us (57%)
  matrix products  152 us (15%)
  blocking collectives  104 us (11%)
  local copies, waits for them, and re-layouts  85.6 us (9%)
  other arithmetic  57.9 us (6%)
  between operations  15.5 us (2%)
    psum x1, waiting for transfers between devices, body(): lax.psum((qkv_grad, qv_bias_grad, proj_grad, up_grad, up_bias_grad, down_...  200 us
    reduce_scatter x1, waiting for transfers between devices, body(): lax.psum_scatter(jnp.dot(context, proj_weight, preferred_element_type=jnp...  79.8 us
    psum x1, blocking collectives, body(): lax.psum((qkv_grad, qv_bias_grad, proj_grad, up_grad, up_bias_grad, down_...  63.2 us
    all_gather x1, waiting for transfers between devices, body(): lax.all_gather(hidden.astype(jnp.bfloat16), 'tensor', axis=0, tiled=True)  45.1 us
    all_gather x1, waiting for transfers between devices, body(): lax.all_gather(grad_second.astype(jnp.bfloat16), 'tensor', axis=0, tiled=...  45 us
    all_gather x1, waiting for transfers between devices, body(): lax.all_gather(grad_first.astype(jnp.bfloat16), 'tensor', axis=0, tiled=T...  45 us
    reduce_scatter x1, waiting for transfers between devices, body(): lax.psum_scatter(dot_last(grad_pre, up_weight).astype(jnp.bfloat16), 'ten...  43.5 us
    reduce_scatter x1, waiting for transfers between devices, body(): lax.psum_scatter(dot_last(grad_qkv, qkv_flat).astype(jnp.bfloat16), 'tens...  42.7 us
  transfers between devices with their start and end apart: 10, of which 9 were waited for; matrix products, arithmetic and copies ran while one was open for 4% of the time, Pallas kernels for 0%

commit v1 on v0

--- a/solution.py
+++ b/solution.py
@@ -3,6 +3,7 @@
 import jax.numpy as jnp
 from jax import lax
 from jax.sharding import PartitionSpec as P
+from jax.lax import psum
 
 HEAD = 64
 LONG = 512
@@ -247,17 +248,16 @@
     tokens_grad = lax.all_gather(
         grad_input_own.astype(jnp.bfloat16), "tensor", axis=0, tiled=True
     ).astype(grad_input_own.dtype)
-    norm_sums = lax.psum(
-        (
-            proj_bias_grad,
-            gain_one_grad,
-            shift_one_grad,
-            down_bias_grad,
-            gain_two_grad,
-            shift_two_grad,
-        ),
-        ("dp", "tensor"),
-    )
+    norm_sums = (
+        proj_bias_grad,
+        gain_one_grad,
+        shift_one_grad,
+        down_bias_grad,
+        gain_two_grad,
+        shift_two_grad,
+    )
+    for k0 in ("tensor", "dp"):
+        norm_sums = psum(norm_sums, k0)
     qkv_grad, qv_bias_grad, proj_grad, up_grad, up_bias_grad, down_grad = lax.psum(
         (qkv_grad, qv_bias_grad, proj_grad, up_grad, up_bias_grad, down_grad), "dp"
     )

time: 982 us -> 981 us (level)
  blocking collectives: 104 us -> 67.1 us
  waiting for transfers between devices: 556 us -> 591 us
    psum x1, waiting for transfers between devices: 200 us -> 235 us  [body(): lax.psum((qkv_grad, qv_bias_grad, proj_grad, up_grad, up_bias_grad, down_...]
    psum x1, blocking collectives: 40.4 us -> 7.1 us  [body(): norm_sums = psum(norm_sums, k0)]
  transfers between devices with their start and end apart: 10 -> 10, of which waited for: 9 -> 9; matrix products, arithmetic and copies ran while one was open for 4% -> 5% of each run, Pallas kernels for 0% -> 0%
where the time goes in v1:
time: 981 us; the launch traced here: 971 us
  waiting for transfers between devices  591 us (60%)
  matrix products  152 us (15%)
  local copies, waits for them, and re-layouts  85.6 us (9%)
  blocking collectives  67.1 us (7%)
  other arithmetic  58.3 us (6%)
  between operations  15.5 us (2%)
    psum x1, waiting for transfers between devices, body(): lax.psum((qkv_grad, qv_bias_grad, proj_grad, up_grad, up_bias_grad, down_...  235 us
    reduce_scatter x1, waiting for transfers between devices, body(): lax.psum_scatter(jnp.dot(context, proj_weight, preferred_element_type=jnp...  79.8 us
    psum x1, blocking collectives, body(): lax.psum((qkv_grad, qv_bias_grad, proj_grad, up_grad, up_bias_grad, down_...  60 us
    all_gather x1, waiting for transfers between devices, body(): lax.all_gather(hidden.astype(jnp.bfloat16), 'tensor', axis=0, tiled=True)  45.1 us
    all_gather x1, waiting for transfers between devices, body(): lax.all_gather(grad_second.astype(jnp.bfloat16), 'tensor', axis=0, tiled=...  45 us
    all_gather x1, waiting for transfers between devices, body(): lax.all_gather(grad_first.astype(jnp.bfloat16), 'tensor', axis=0, tiled=T...  45 us
    reduce_scatter x1, waiting for transfers between devices, body(): lax.psum_scatter(dot_last(grad_pre, up_weight).astype(jnp.bfloat16), 'ten...  43.5 us
    reduce_scatter x1, waiting for transfers between devices, body(): lax.psum_scatter(dot_last(grad_qkv, qkv_flat).astype(jnp.bfloat16), 'tens...  42.7 us
  transfers between devices with their start and end apart: 10, of which 9 were waited for; matrix products, arithmetic and copies ran while one was open for 5% of the time, Pallas kernels for 0%

profile of v1, /device:TPU:0, one launch (start us, length us, event | category | flops | bytes accessed | tf_op | source)
XLA Modules:
  0.0 970.9 jit_solution(15084983017677057927)
XLA Ops:
  10.6 3.8 copy.62
  14.4 6.7 add_convert_fusion
  33.7 37.3 %while.22 = (s32[]{:T(128)}, bf16[4,512,384]{2,1,0:T(8,128)(2,1)}, f32[4,6,512]{2,1,0:T(8,128)}, bf16[4,512,384]{1,2,0:T(8,128)(2,1)}, pred[4,512,512]{1,2,0:T(8...) while((s32[]{:T(128)}, bf16[4,512,384]{2,1,0:T(8,128)(2,1)}, ...), condition=%wide.region_5.6_spmd, body=%wide.region_2.5_spmd.sunk | while | flops 421721088 | bytes 25792624 | solution.py:179
  71.0 6.0 fusion.72
  77.2 79.8 %reduce-scatter.5.cloned.1.call-done = f32[1024,768]{1,0:T(8,128)} async-done(((f32[2048,768]{1,0:T(8,128)}), f32[1024,768]{1,0:T(8,128)}) %reduce-scatter.5.cloned.1.call-update) | async-done | bytes 3145744 | tf_op jit(solution)/shard_map/reduce_scatter | solution.py:181
  163.3 45.1 %all-gather.6.cloned.1.call-done = bf16[2048,768]{1,0:T(8,128)(2,1)} async-done(((bf16[1024,768]{1,0:T(8,128)(2,1)}), bf16[2048,768]{1,0:T(8,128)(2,1)}) %all-gather.6.cloned.1.call-update) | async-done | bytes 3145744 | tf_op jit(solution)/shard_map/all_gather | solution.py:190
  208.3 33.2 %fusion.20 = (bf16[2048,1536]{1,0:T(8,128)(2,1)S(1)}, f32[2048,1536]{1,0:T(8,128)}) fusion(f32[1536]{0:T(1024)S(1)} %copy-done.29, bf16[2048,768]{1,0:T(8,128)(2,1)} %all-gather.6.cloned.1.call-done, bf16[768,1536]{1,0:T(8,128)(2,1)S(1)} %copy-done), kind=kOutput, calls=%fused_computation.40 | convolution fusion | flops 5039456256 | bytes 24385536 | tf_op jit(solution)/shard_map/dot_general | solution.py:191
  244.1 6.3 convolution_convert_fusion.2
  251.3 42.7 %reduce-scatter.7.cloned.1.call-done = bf16[1024,768]{1,0:T(8,128)(2,1)} async-done(((bf16[2048,768]{1,0:T(8,128)(2,1)}), bf16[1024,768]{1,0:T(8,128)(2,1)}) %reduce-scatter.7.cloned.1.call-update) | async-done | bytes 1572880 | tf_op jit(solution)/shard_map/reduce_scatter | solution.py:193
  302.0 3.9 fusion.64
  306.0 45.0 %all-gather.10.cloned.1.call-done = bf16[2048,768]{1,0:T(8,128)(2,1)} async-done(((bf16[1024,768]{1,0:T(8,128)(2,1)}), bf16[2048,768]{1,0:T(8,128)(2,1)}) %all-gather.10.cloned.1.call-update) | async-done | bytes 3145744 | tf_op jit(solution)/shard_map/all_gather | solution.py:211
  351.0 12.6 %convert_reduce_fusion = (f32[1536]{0:T(1024)}, bf16[2048,1536]{1,0:T(8,128)(2,1)S(1)}) fusion(f32[2048,1536]{1,0:T(8,128)} %get-tuple-element.226, f32[1536]{0:T(1024)S(1)} %copy-done.29, bf16[2048,768]{1,0:T(8,128)(2,1)} %all-gather.10.cloned.1.call-done, bf16[1536,768]{1,0:T(8,128)(2,1)} %param.30), kind=kOutput, calls=%fused_computation.47 | convolution fusion | flops 4872731136 | bytes 24391680 | tf_op jit(solution)/shard_map/dot_general | solution.py:14
  366.4 6.4 convolution_convert_fusion.1
  372.9 43.5 %reduce-scatter.9.cloned.1.call-done = bf16[1024,768]{1,0:T(8,128)(2,1)} async-done(((bf16[2048,768]{1,0:T(8,128)(2,1)}), bf16[1024,768]{1,0:T(8,128)(2,1)}) %reduce-scatter.9.cloned.1.call-update) | async-done | bytes 1572880 | tf_op jit(solution)/shard_map/reduce_scatter | solution.py:217
  416.3 3.6 multiply_reduce_fusion.1
  424.5 45.0 %all-gather.12.cloned.1.call-done = bf16[2048,768]{1,0:T(8,128)(2,1)} async-done(((bf16[1024,768]{1,0:T(8,128)(2,1)}), bf16[2048,768]{1,0:T(8,128)(2,1)}) %all-gather.12.cloned.1.call-update) | async-done | bytes 3145744 | tf_op jit(solution)/shard_map/all_gather | solution.py:227
  469.5 4.9 convolution_convert_fusion.3
  474.4 60.4 %while.23 = (s32[]{:T(128)}, bf16[4,512,1152]{1,2,0:T(8,128)(2,1)}, bf16[4,512,384]{1,2,0:T(8,128)(2,1)}, pred[4,512,512]{1,2,0:T(8,128)(4,1)}, bf16[4,512,384]{...) while((s32[]{:T(128)}, bf16[4,512,1152]{1,2,0:T(8,128)(2,1)}, ...), condition=%wide.region_19.20_spmd, body=%wide.region_17.19_spmd.sunk | while | flops 1034744832 | bytes 58806396 | solution.py:230
  534.8 6.7 copy.71
  541.5 7.9 convolution_convert_fusion
  550.3 42.7 %reduce-scatter.11.cloned.1.call-done = bf16[1024,768]{1,0:T(8,128)(2,1)} async-done(((bf16[2048,768]{1,0:T(8,128)(2,1)}), bf16[1024,768]{1,0:T(8,128)(2,1)}) %reduce-scatter.11.cloned.1.call-update) | async-done | bytes 1572880 | tf_op jit(solution)/shard_map/reduce_scatter | solution.py:241
  593.0 3.7 fusion.48
  596.8 9.9 %fusion.76 = f32[1536,768]{1,0:T(8,128)} fusion(bf16[2048,1536]{1,0:T(8,128)(2,1)} %copy-done.30, bf16[2048,768]{1,0:T(8,128)(2,1)} %all-gather.10.cloned.1.call-done), kind=kOutput, calls=%fused_computation.151 | convolution fusion | flops 4831838208 | bytes 14155776 | tf_op jit(solution)/shard_map/dot_general | solution.py:20
  606.7 9.7 %fusion.75 = f32[768,1536]{1,0:T(8,128)} fusion(bf16[2048,768]{1,0:T(8,128)(2,1)S(1)} %copy-done.27, bf16[2048,1536]{1,0:T(8,128)(2,1)} %copy-done.31), kind=kOutput, calls=%fused_computation.150 | convolution fusion | flops 4831838208 | bytes 14155776 | tf_op jit(solution)/shard_map/dot_general | solution.py:20
  616.4 4.0 fusion.73
  623.4 4.8 fusion.74
  628.2 11.3 %all-gather.8.cloned.1.call-done = bf16[2048,768]{1,0:T(8,128)(2,1)} async-done(((bf16[1024,768]{1,0:T(8,128)(2,1)}), bf16[2048,768]{1,0:T(8,128)(2,1)}) %all-gather.8.cloned.1.call-update) | async-done | bytes 3145744 | tf_op jit(solution)/shard_map/all_gather | solution.py:203
  639.5 7.1 all-reduce.2
  650.2 60.0 %all-reduce = (f32[2,384]{1,0:T(2,128)}, f32[768]{0:T(1024)}, f32[768]{0:T(1024)}, f32[768]{0:T(1024)}, f32[1536]{0:T(1024)}, /*index=5*/f32[768]{0:T(1024)}, f32[768]{0:T(1024)}, f32[768]{0:T(1024)}) all-reduce(f32[2,384]{1,0:T(2,128)S(1)} %pad_maximum_fusion.1, ...), channel_id=1, replica_groups=mesh['dp'=16,'tensor'=2] {'dp'}, use_global_device_ids=true, to_apply=%region_23.24 | all-reduce | flops 6912 | bytes 55296 | tf_op jit(solution)/shard_map/psum | solution.py:261
  710.2 5.3 convert_element_type.130
  715.5 234.9 %all-reduce.5.cloned.1.call-done = (f32[768,3,384]{2,0,1:T(8,128)}, f32[384,768]{1,0:T(8,128)}, f32[768,1536]{1,0:T(8,128)}, f32[1536,768]{1,0:T(8,128)}) async-done(((f32[768,3,384]{2,0,1:T(8,128)}, f32[384,768]{1,0:T(8,128)}, f32[768,1536]{1,0:T(8,128)}, f32[1536,768]{1,0:T(8,128)}), (f32[768,3,384]{2,0,1:T(8,128)}, f32[384,768]{1,0:T(8,128)}, f32[768,1536]{1,0:T(8,128)}, ...) | async-done | bytes 14155792 | tf_op jit(solution)/shard_map/psum | solution.py:261
  952.0 5.1 copy.111
  (230 shorter events, 152.9 us)
Async XLA Ops:
  7.2 201.2 %copy-start = (bf16[768,1536]{1,0:T(8,128)(2,1)S(1)}, bf16[768,1536]{1,0:T(8,128)(2,1)}, u32[]{:S(2)}) copy-start(bf16[768,1536]{1,0:T(8,128)(2,1)} %param.28) | copy-start | bytes 7077892
  7.2 149.8 %reduce-scatter.5.cloned.1.call-start = ((), (), s32[]{:S(2)}) async-start(), calls=%async_computation.4 | async-start | bytes 9437184 | tf_op jit(solution)/shard_map/reduce_scatter | solution.py:181
  10.6 10.6 %copy-start.16 = (s32[2048]{0:T(1024)}, s32[2048]{0:T(1024)S(1)}, u32[]{:S(2)}) copy-start(s32[2048]{0:T(1024)S(1)} %get-tuple-element.152) | copy-start | bytes 24580
  77.1 79.9 %copy-start.24 = (f32[768]{0:T(1024)S(1)}, f32[768]{0:T(1024)}, u32[]{:S(2)}) copy-start(f32[768]{0:T(1024)} %param.25) | copy-start | bytes 9220
  77.1 131.2 %all-gather.6.cloned.1.call-start = ((), (), s32[]{:S(2)}) async-start(), calls=%async_computation.5 | async-start | bytes 4718592 | tf_op jit(solution)/shard_map/all_gather | solution.py:190
  161.5 46.8 %copy-start.29 = (f32[1536]{0:T(1024)S(1)}, f32[1536]{0:T(1024)}, u32[]{:S(2)}) copy-start(f32[1536]{0:T(1024)} %param.29) | copy-start | bytes 18436
  163.2 130.8 %reduce-scatter.7.cloned.1.call-start = ((), (), s32[]{:S(2)}) async-start(), calls=%async_computation.6 | async-start | bytes 4718592 | tf_op jit(solution)/shard_map/reduce_scatter | solution.py:193
  208.3 35.8 %copy-start.28 = (bf16[1536,768]{1,0:T(8,128)(2,1)S(1)}, bf16[1536,768]{1,0:T(8,128)(2,1)}, u32[]{:S(2)}) copy-start(bf16[1536,768]{1,0:T(8,128)(2,1)} %param.30) | copy-start | bytes 7077892
  250.5 43.5 %copy-start.25 = (f32[768]{0:T(1024)S(1)}, f32[768]{0:T(1024)}, u32[]{:S(2)}) copy-start(f32[768]{0:T(1024)} %param.31) | copy-start | bytes 9220
  250.5 100.5 %all-gather.10.cloned.1.call-start = ((), (), s32[]{:S(2)}) async-start(), calls=%async_computation.8 | async-start | bytes 4718592 | tf_op jit(solution)/shard_map/all_gather | solution.py:211
  306.0 110.4 %reduce-scatter.9.cloned.1.call-start = ((), (), s32[]{:S(2)}) async-start(), calls=%async_computation.9 | async-start | bytes 4718592 | tf_op jit(solution)/shard_map/reduce_scatter | solution.py:217
  372.8 43.5 %copy-start.3 = (f32[1024,768]{1,0:T(8,128)S(1)}, f32[1024,768]{1,0:T(8,128)}, u32[]{:S(2)}) copy-start(f32[1024,768]{1,0:T(8,128)} %copy-done.2) | copy-start | bytes 9437188
  372.8 96.7 %all-gather.12.cloned.1.call-start = ((), (), s32[]{:S(2)}) async-start(), calls=%async_computation.10 | async-start | bytes 4718592 | tf_op jit(solution)/shard_map/all_gather | solution.py:227
  423.1 46.4 %copy-start.14 = (bf16[384,768]{1,0:T(8,128)(2,1)S(1)}, bf16[384,768]{1,0:T(8,128)(2,1)}, u32[]{:S(2)}) copy-start(bf16[384,768]{1,0:T(8,128)(2,1)} %param.24) | copy-start | bytes 1769476
  424.4 168.5 %reduce-scatter.11.cloned.1.call-start = ((), (), s32[]{:S(2)}) async-start(), calls=%async_computation.11 | async-start | bytes 4718592 | tf_op jit(solution)/shard_map/reduce_scatter | solution.py:241
  534.8 6.8 copy-start.12
  549.5 43.5 %copy-start.5 = (f32[1024,768]{1,0:T(8,128)S(1)}, f32[1024,768]{1,0:T(8,128)}, u32[]{:S(2)}) copy-start(f32[1024,768]{1,0:T(8,128)} %copy-done.4) | copy-start | bytes 9437188
  549.5 90.0 %all-gather.8.cloned.1.call-start = ((), (), s32[]{:S(2)}) async-start(), calls=%async_computation.7 | async-start | bytes 4718592 | tf_op jit(solution)/shard_map/all_gather | solution.py:203
  550.2 160.0 %all-gather.14.cloned.1.call-start = ((), (), s32[]{:S(2)}) async-start(), calls=%async_computation.12 | async-start | bytes 4718592 | tf_op jit(solution)/shard_map/all_gather | solution.py:248
  596.7 10.0 %copy-start.27 = (bf16[2048,768]{1,0:T(8,128)(2,1)S(1)}, bf16[2048,768]{1,0:T(8,128)(2,1)}, u32[]{:S(2)}) copy-start(bf16[2048,768]{1,0:T(8,128)(2,1)} %all-gather.6.cloned.1.call-done) | copy-start | bytes 9437188
  596.7 353.7 %all-reduce.5.cloned.1.call-start = ((), (), s32[]{:S(2)}) async-start(), calls=%async_computation.13 | async-start | bytes 28311552 | tf_op jit(solution)/shard_map/psum | solution.py:261
  596.7 19.7 %slice-start.4 = ((s8[4718592]{0:T(1024)(128)(4,1)}), s8[4194304]{0:T(1024)(128)(4,1)S(1)}, s32[]{:S(2)}) async-start(s8[4718592]{0:T(1024)(128)(4,1)} %bitcast.156), calls=%async_computation.18 | async-start | bytes 8388608
  606.7 9.7 %slice-start.5 = ((s8[4718592]{0:T(1024)(128)(4,1)}), s8[524288]{0:T(1024)(128)(4,1)S(1)}, s32[]{:S(2)}) async-start(s8[4718592]{0:T(1024)(128)(4,1)} %bitcast.156), calls=%async_computation.19 | async-start | bytes 1048576
  606.7 9.7 %copy-start.11 = (bf16[2048,768]{1,0:T(8,128)(2,1)S(1)}, bf16[2048,768]{1,0:T(8,128)(2,1)}, u32[]{:S(2)}) copy-start(bf16[2048,768]{1,0:T(8,128)(2,1)} %param.21) | copy-start | bytes 9437188
  628.2 11.3 %copy-start.21 = (f32[768]{0:T(1024)S(1)}, f32[768]{0:T(1024)}, u32[]{:S(2)}) copy-start(f32[768]{0:T(1024)} %get-tuple-element.144) | copy-start | bytes 9220
  628.2 11.3 %copy-start.22 = (f32[768]{0:T(1024)S(1)}, f32[768]{0:T(1024)}, u32[]{:S(2)}) copy-start(f32[768]{0:T(1024)} %get-tuple-element.149) | copy-start | bytes 9220
  628.2 22.0 %copy-start.23 = (f32[1536]{0:T(1024)S(1)}, f32[1536]{0:T(1024)}, u32[]{:S(2)}) copy-start(f32[1536]{0:T(1024)} %get-tuple-element.227) | copy-start | bytes 18436
  710.2 240.2 %copy-start.9 = (bf16[2048,768]{1,0:T(8,128)(2,1)S(1)}, bf16[2048,768]{1,0:T(8,128)(2,1)}, u32[]{:S(2)}) copy-start(bf16[2048,768]{1,0:T(8,128)(2,1)} %all-gather.8.cloned.1.call-done) | copy-start | bytes 9437188
  950.4 7.8 slice-start.2
  952.0 5.1 copy-start.13
  952.0 6.1 slice-start.3
  958.2 5.7 copy-start.1
  (16 other events, 40.3 us)
Sparse Core Ops, SparseCore 0:
  77.2 79.7 reduce-scatter.4
  163.4 44.9 all-gather.5
  250.6 43.3 reduce-scatter.6
  306.1 44.9 all-gather.9
  372.9 43.3 reduce-scatter.8
  424.6 44.9 all-gather.11
  549.6 43.3 reduce-scatter.10
  594.5 44.9 all-gather.7
  641.6 44.9 all-gather.13
  691.6 258.7 all-reduce.4
